TPU v7x, 32 devices: a whole 2x2x4 slice. The times are simulated.
32 devices in a mesh: req: 8 (over z, y), tp: 4 (over x, core).
Axes of the slice: x: 2, y: 2, z: 4, core: 2. Of those that a mesh axis runs over, the one named last changes fastest.
Arguments:
- tokens: bfloat16 [16, 256, 2048], P('req'), may hold values from -6 to 6
- attn_gain: float32 [2048], replicated, may hold values from 0.25 to 1.75
- w_query: bfloat16 [2048, 1280], P(None, 'tp'), may hold values from -0.125 to 0.125
- key_value_weight: bfloat16 [2048, 640], replicated, may hold values from -0.125 to 0.125
- w_out: bfloat16 [1280, 2048], P('tp'), may hold values from -0.15625 to 0.15625
- q_gain: float32 [64], replicated, as said below
- k_gain: float32 [64], replicated, as said below
- stored: bfloat16 [8, 5, 2048, 128], P('req'), may hold values from -6 to 6
- continuing: int32 [16], replicated, may hold values from 0 to 1, as said below
- cache_row: int32 [16], replicated, may hold values from -1 to 7, as said below
- cache_len: int32 [16], replicated, may hold values from 0 to 2048, as said below
Outputs:
- layer: bfloat16 [16, 256, 2048], P('req')
- decoding_group_cache: bfloat16 [32, 5, 1152, 128], P('req', None, 'tp')
Inputs may be any that keep to these rules, and one draw needn't show every extreme that they name: `continuing`: exactly 8 requests have 1. `cache_row`: a continuing request's row of stored; every row belongs to exactly one continuing request; -1 for the others. `cache_len`: 1 to 2048 for a continuing request, 2048 for at least one; 0 for the others. `q_gain`: positive. `k_gain`: positive.
All inputs are finite; a program needn't handle non-finite values.
Results may differ from a plain program's by a relative error of at most 0.005.
The roundings to bfloat16 on the way count: a program that leaves them out, or rounds other values in their place, can miss the bound.
Values may be sent and summed in bfloat16 or wider, within the bound.
No kernel may reach another device: no remote copies, remote signals or barrier semaphores. Data moves between devices by JAX's collectives and lax.ppermute only.
A program may use at most 128 MiB of HBM per device.

v0:
```python
import math
import jax
import jax.numpy as jnp
from jax import lax
from jax.sharding import PartitionSpec as P


def swapped(value, axis, apart):
    mask = 2**apart
    pairs = [(source, source ^ mask) for source in range(lax.axis_size(axis))]
    return lax.ppermute(value, axis, pairs)


def normalize(values, gain):
    return values * lax.rsqrt(jnp.mean(values * values, axis=-1, keepdims=True) + 1e-06) * gain


def rotary(values, positions):
    half_dim = values.shape[-1] // 2
    freq = jnp.exp(
        -math.log(10000.0) * jnp.arange(half_dim).astype(jnp.float32) * 2.0 / values.shape[-1]
    )
    angle = positions.astype(jnp.float32)[..., None] * freq
    cosine = jnp.cos(angle)[..., None, :]
    sine = jnp.sin(angle)[..., None, :]
    first_half = values[..., :half_dim]
    second_half = values[..., half_dim:]
    return jnp.concatenate(
        [first_half * cosine - second_half * sine, second_half * cosine + first_half * sine],
        axis=-1,
    )


def attend(query_one, keys_one, allowed, head_dim, new_count, scale):
    scores = (
        jnp.einsum(
            "hqd,hkd->hqk", query_one, keys_one[..., :head_dim], preferred_element_type=jnp.float32
        )
        * scale
    )
    scores = jnp.where(allowed[None], scores, -jnp.inf)
    row_max = jnp.max(scores, axis=-1, keepdims=True)
    weights = jnp.exp(scores - row_max)
    probs = (weights / jnp.sum(weights, axis=-1, keepdims=True)).astype(jnp.bfloat16)
    mixed = jnp.einsum(
        "hqk,hkd->qhd", probs, keys_one[..., head_dim:], preferred_element_type=jnp.float32
    )
    return mixed.astype(jnp.bfloat16).reshape(new_count, query_one.shape[0] * head_dim)


def on_device(
    tokens,
    attn_gain,
    w_query,
    key_value_weight,
    w_out,
    q_gain,
    k_gain,
    stored,
    continuing,
    cache_row,
    cache_len,
):
    tp_count = lax.axis_size("tp")
    req_place = lax.axis_index("req")
    tp_place = lax.axis_index("tp")
    req_dev, new_count, width = tokens.shape
    head_dim = q_gain.shape[0]
    kv_heads = key_value_weight.shape[1] // (2 * head_dim)
    local_heads = w_query.shape[1] // head_dim
    query_group_ratio = local_heads * tp_count // kv_heads
    cache_span = stored.shape[2]
    total_length = cache_span + new_count
    scale = 1.0 / math.sqrt(head_dim)
    relayed = lax.all_to_all(stored, "req", split_axis=2, concat_axis=0, tiled=True)
    live_all = continuing == 1
    rows_all = jnp.where(live_all, cache_row, 0)
    select_chosen = jnp.take(relayed, rows_all, axis=0)
    stored_entries = lax.all_to_all(
        jnp.where(live_all[:, None, None, None], select_chosen, jnp.zeros_like(select_chosen)),
        "req",
        split_axis=0,
        concat_axis=2,
        tiled=True,
    )
    first = req_place * req_dev
    my_live = lax.dynamic_slice_in_dim(continuing, first, req_dev) == 1
    my_len = jnp.where(my_live, lax.dynamic_slice_in_dim(cache_len, first, req_dev), 0)
    position = jnp.arange(cache_span, dtype=jnp.int32)
    stored_entries = jnp.where(
        (position[None, :] < my_len[:, None])[:, None, :, None],
        stored_entries,
        jnp.zeros_like(stored_entries),
    )
    token_rows = tokens.reshape(req_dev * new_count, width)
    normalized_input = normalize(token_rows.astype(jnp.float32), attn_gain).astype(jnp.bfloat16)
    positions = my_len[:, None] + jnp.arange(new_count, dtype=jnp.int32)[None, :]
    query = jnp.dot(normalized_input, w_query, preferred_element_type=jnp.float32).reshape(
        req_dev, new_count, local_heads, head_dim
    )
    query = rotary(normalize(query, q_gain), positions).astype(jnp.bfloat16)
    key_value_rows = jnp.dot(
        normalized_input, key_value_weight, preferred_element_type=jnp.float32
    ).reshape(req_dev, new_count, kv_heads, 2 * head_dim)
    keys_new = rotary(normalize(key_value_rows[..., :head_dim], k_gain), positions)
    fresh = jnp.concatenate([keys_new, key_value_rows[..., head_dim:]], axis=-1).astype(
        jnp.bfloat16
    )
    fresh = jnp.transpose(fresh, (0, 2, 1, 3))
    keys_all = jnp.concatenate([stored_entries, fresh], axis=2)
    head_select = (
        tp_place * local_heads + jnp.arange(local_heads, dtype=jnp.int32)
    ) // query_group_ratio
    query_index = jnp.arange(new_count, dtype=jnp.int32)[:, None]
    key_index = jnp.arange(total_length, dtype=jnp.int32)[None, :]
    outputs = []
    for number in range(req_dev):
        query_one = jnp.transpose(query[number], (1, 0, 2))
        chosen = jnp.take(keys_all[number], head_select, axis=0)
        allowed = jnp.where(
            key_index < cache_span,
            key_index < my_len[number],
            key_index - cache_span <= query_index,
        )
        mixed = attend(query_one, chosen, allowed, head_dim, new_count, scale)
        outputs.append(mixed)
    mixed_all = jnp.concatenate(outputs, axis=0)
    summed = lax.psum(jnp.dot(mixed_all, w_out, preferred_element_type=jnp.float32), "tp")
    layer = (token_rows.astype(jnp.float32) + summed).astype(jnp.bfloat16)
    layer = layer.reshape(req_dev, new_count, width)
    padded_tokens = jnp.concatenate(
        [stored_entries, jnp.zeros((req_dev, kv_heads, new_count, 2 * head_dim), jnp.bfloat16)],
        axis=2,
    )
    whole = jax.vmap(
        lambda padded_one, fresh_one, offset: lax.dynamic_update_slice_in_dim(
            padded_one, fresh_one, offset, 1
        )
    )(padded_tokens, fresh, my_len)
    half_span = total_length // 2
    segment = half_span // tp_count
    pair_side = req_place % 2
    kept_half = lax.dynamic_slice_in_dim(
        whole, pair_side * half_span + tp_place * segment, segment, 2
    )
    sent_half = lax.dynamic_slice_in_dim(
        whole, (1 - pair_side) * half_span + tp_place * segment, segment, 2
    )
    partner = swapped(sent_half, "req", 0)
    decoding_group_cache = jnp.where(
        pair_side == 0,
        jnp.concatenate([kept_half, partner], axis=0),
        jnp.concatenate([partner, kept_half], axis=0),
    )
    return (layer, decoding_group_cache)


def solution(mesh):
    return jax.shard_map(
        on_device,
        mesh=mesh,
        in_specs=(
            P("req", None, None),
            P(),
            P(None, "tp"),
            P(),
            P("tp", None),
            P(),
            P(),
            P("req", None, None, None),
            P(),
            P(),
            P(),
        ),
        out_specs=(P("req", None, None), P("req", None, "tp", None)),
        check_vma=False,
    )
```

profile of v0, /device:TPU:0, one launch (start us, length us, event | category | flops | bytes accessed | tf_op | source)
XLA Modules:
  0.0 405.0 jit_solution(1439324511392412007)
XLA Ops:
  7.2 5.2 %copy.40 = bf16[1,5,2048,128]{3,1,0,2:T(8,128)(2,1)} copy(bf16[1,5,2048,128]{3,2,1,0:T(8,128)(2,1)} %param.20) | data formatting | bytes 5242880 | tf_op args[7]
  12.4 7.4 %all-to-all-start = ((bf16[1,5,2048,128]{3,1,0,2:T(8,128)(2,1)}), bf16[1,5,2048,128]{3,1,0,2:T(8,128)(2,1)}, u32[]{:S(2)}, u32[]{:S(2)}) async-start(bf16[1,5,2048,128]{3,1,0,2:T(8,128)(2,1)} %copy.40), calls=%async_computation | async-start | bytes 8388608 | tf_op jit(solution)/shard_map/all_to_all | solution.py:75
  19.9 93.2 %all-to-all-done = bf16[1,5,2048,128]{3,1,0,2:T(8,128)(2,1)} async-done(((bf16[1,5,2048,128]{3,1,0,2:T(8,128)(2,1)}), bf16[1,5,2048,128]{3,1,0,2:T(8,128)(2,1)}, u32[]{:S(2)}, u32[]{:S(2)}) %all-to-all-start) | async-done | bytes 2621472 | tf_op jit(solution)/shard_map/all_to_all | solution.py:75
  113.1 4.4 %copy.54 = bf16[1,5,8,256,128]{4,3,1,2,0:T(8,128)(2,1)} copy(bf16[1,5,8,256,128]{4,1,3,2,0:T(8,128)(2,1)} %bitcast.1) | data formatting | bytes 5242880 | tf_op jit(solution)/shard_map/all_to_all | solution.py:75
  117.6 5.3 %gather_fusion = bf16[16,5,256,128]{3,2,1,0:T(8,128)(2,1)} fusion(bf16[8,5,256,128]{3,2,1,0:T(8,128)(2,1)} %bitcast.95, s32[1024]{0:T(1024)S(1)} %pad_clamp_fusion.1), kind=kCustom, calls=%fused_computation.2 | custom fusion | bytes 10485824 | tf_op jit(solution)/shard_map/jit(_take)/gather | solution.py:78
  122.9 5.5 %select_select_fusion = bf16[16,5,256,128]{3,2,1,0:T(8,128)(2,1)} fusion(bf16[16,5,256,128]{3,2,1,0:T(8,128)(2,1)} %gather_fusion, pred[16]{0:T(512)(128)(4,1)S(1)} %get-tuple-element.41, pred[16]{0:T(512)(128)(4,1)S(1)} %get-tuple-element.65), kind=kLoop, calls=%fused_computation.27 | loop fusion | flops 5242880 | bytes 10485792 | tf_op jit(solution)/shard_map/jit(_where)/select_n | solution.py:80
  128.3 4.6 %all-to-all-start.1 = ((bf16[16,5,256,128]{3,2,1,0:T(8,128)(2,1)}), bf16[16,5,256,128]{3,2,1,0:T(8,128)(2,1)}, u32[]{:S(2)}, u32[]{:S(2)}) async-start(bf16[16,5,256,128]{3,2,1,0:T(8,128)(2,1)} %select_select_fusion), calls=%async_computation.1 | async-start | bytes 10485760 | tf_op jit(solution)/shard_map/all_to_all | solution.py:79
  133.2 4.6 %copy.44 = bf16[2048,640]{0,1:T(8,128)(2,1)} copy(bf16[2048,640]{1,0:T(8,128)(2,1)} %param.16) | data formatting | bytes 5242880 | tf_op args[3]
  138.3 3.4 fusion.45
  151.3 96.6 %all-to-all-done.1 = bf16[16,5,256,128]{3,2,1,0:T(8,128)(2,1)} async-done(((bf16[16,5,256,128]{3,2,1,0:T(8,128)(2,1)}), bf16[16,5,256,128]{3,2,1,0:T(8,128)(2,1)}, u32[]{:S(2)}, u32[]{:S(2)}) %all-to-all-start.1) | async-done | bytes 5242912 | tf_op jit(solution)/shard_map/all_to_all | solution.py:79
  252.0 4.1 %fusion.14 = (bf16[5,2304,128]{2,1,0:T(8,128)(2,1)}, bf16[5,2304,128]{2,1,0:T(8,128)(2,1)}) fusion(bf16[2,5,2048,128]{3,2,1,0:T(8,128)(2,1)S(1)} %bitcast_select_fusion, bf16[2,5,256,128]{3,2,1,0:T(8,128)(2,1)S(1)} %copy.45), kind=kLoop, calls=%fused_computation.33 | loop fusion | flops 11796480 | bytes 11796480 | tf_op jit(solution)/shard_map/squeeze | solution.py:119
  256.1 4.6 %gather_fusion.1 = bf16[5,2304,128]{2,1,0:T(8,128)(2,1)} fusion(bf16[5,2304,128]{2,1,0:T(8,128)(2,1)} %get-tuple-element.49, s32[1024]{0:T(1024)S(1)} %pad_clamp_fusion), kind=kCustom, calls=%fused_computation.clone | custom fusion | bytes 5898260 | tf_op jit(solution)/shard_map/jit(_take)/gather | solution.py:119
  260.7 5.4 %copy.46 = bf16[5,2304,128]{1,2,0:T(8,128)(2,1)} copy(bf16[5,2304,128]{2,1,0:T(8,128)(2,1)} %gather_fusion.1) | data formatting | bytes 5898240 | tf_op jit(solution)/shard_map/jit(_take)/gather | solution.py:119
  266.1 4.6 %gather_fusion.2 = bf16[5,2304,128]{2,1,0:T(8,128)(2,1)} fusion(bf16[5,2304,128]{2,1,0:T(8,128)(2,1)} %get-tuple-element.50, s32[1024]{0:T(1024)S(1)} %pad_clamp_fusion), kind=kCustom, calls=%fused_computation.1.clone | custom fusion | bytes 5898260 | tf_op jit(solution)/shard_map/jit(_take)/gather | solution.py:119
  270.8 5.4 %copy.47 = bf16[5,2304,128]{1,2,0:T(8,128)(2,1)} copy(bf16[5,2304,128]{2,1,0:T(8,128)(2,1)} %gather_fusion.2) | data formatting | bytes 5898240 | tf_op jit(solution)/shard_map/jit(_take)/gather | solution.py:119
  276.2 5.8 %broadcast_select_fusion.1 = (bf16[5,2304,128]{1,2,0:T(8,128)(2,1)}, bf16[5,2304,128]{1,2,0:T(8,128)(2,1)}) fusion(bf16[5,2304,128]{1,2,0:T(8,128)(2,1)} %copy.46, pred[5]{0:T(512)(128)(4,1)S(1)} %compare_and_fusion, bf16[5,2304,128]{1,2,0:T(8,128)(2,1)} %copy.47), kind=kLoop, calls=%fused_computation.37 | loop fusion | flops 2949120 | bytes 11796485 | tf_op jit(solution)/shard_map/jit(_take)/select_n | solution.py:119
  282.0 5.2 %fusion.90 = f32[5,256]{1,0:T(8,128)S(1)} fusion(pred[256,2304]{1,0:T(8,128)(4,1)S(1)} %get-tuple-element.58, bf16[5,2304,128]{1,2,0:T(8,128)(2,1)} %get-tuple-element.62, bf16[2,256,5,32]{1,3,2,0:T(8,128)(2,1)S(1)} %get-tuple-element.52, bf16[2,256,5,32]{1,3,2,0:T(8,128)(2,1)S(1)} %get-tuple-element.51), kind=kOutput, calls=%fused_computation.119 | convolution fusion | flops 389613824 | bytes 2397184 | tf_op jit(solution)/shard_map/sub | solution.py:43
  287.2 7.0 %fusion.37 = bf16[5,64,256]{2,1,0:T(8,128)(2,1)} fusion(f32[5,256]{1,0:T(8,128)S(1)} %fusion.90, bf16[5,2304,128]{1,2,0:T(8,128)(2,1)} %get-tuple-element.62, pred[256,2304]{1,0:T(8,128)(4,1)S(1)} %get-tuple-element.58, bf16[2,256,5,32]{1,3,2,0:T(8,128)(2,1)S(1)} %get-tuple-element.52, bf16[2,256,5,32]{1,3,2,0:T(8,128)(2,1)S(1)} %get-tuple-element.51), kind=kOutput, calls=%fused_computation.54 | convolution fusion | flops 770133504 | bytes 4035584 | tf_op jit(solution)/shard_map/hqk,hkd->qhd/dot_general | solution.py:45
  294.2 5.5 %fusion.95 = f32[5,256]{1,0:T(8,128)S(1)} fusion(pred[256,2304]{1,0:T(8,128)(4,1)S(1)} %get-tuple-element.57, bf16[5,2304,128]{1,2,0:T(8,128)(2,1)} %get-tuple-element.61, bf16[2,256,5,32]{1,3,2,0:T(8,128)(2,1)S(1)} %get-tuple-element.51, bf16[2,256,5,32]{1,3,2,0:T(8,128)(2,1)S(1)} %get-tuple-element.52), kind=kOutput, calls=%fused_computation.120 | convolution fusion | flops 389613824 | bytes 2397184 | tf_op jit(solution)/shard_map/sub | solution.py:43
  299.6 6.3 %fusion.40 = bf16[5,64,256]{2,1,0:T(8,128)(2,1)S(1)} fusion(f32[5,256]{1,0:T(8,128)S(1)} %fusion.95, bf16[5,2304,128]{1,2,0:T(8,128)(2,1)} %get-tuple-element.61, pred[256,2304]{1,0:T(8,128)(4,1)S(1)} %get-tuple-element.57, bf16[2,256,5,32]{1,3,2,0:T(8,128)(2,1)S(1)} %get-tuple-element.51, bf16[2,256,5,32]{1,3,2,0:T(8,128)(2,1)S(1)} %get-tuple-element.52), kind=kOutput, calls=%fused_computation.55 | convolution fusion | flops 770133504 | bytes 4035584 | tf_op jit(solution)/shard_map/hqk,hkd->qhd/dot_general | solution.py:45
  306.0 3.3 fusion.47
  310.1 5.6 %concatenate.30 = bf16[2,5,2304,128]{3,2,1,0:T(8,128)(2,1)} pad(bf16[2,5,2048,128]{3,2,1,0:T(8,128)(2,1)} %copy-done.1, bf16[]{:T(256)} %constant.52.clone.1), padding=0_0x0_0x0_256x0_0 | pad | bytes 11141122 | tf_op jit(solution)/shard_map/concatenate | solution.py:131
  315.7 24.9 %while.1 = (s32[]{:T(128)}, bf16[2,5,2304,128]{3,2,1,0:T(8,128)(2,1)}, s32[2,4]{1,0:T(2,128)S(1)}, bf16[2,5,256,128]{3,2,1,0:T(8,128)(2,1)S(1)}, s32[]{:T(128)}, /*index=5*/s32[4]{0:T(128)S(1)}, s32[]{:T(128)}) while((s32[]{:T(128)}, bf16[2,5,2304,128]{3,2,1,0:T(8,128)(2,1)}, s32[2,4]{1,0:T(2,128)S(1)}, bf16[2,5,256,128]{3,2,1,0:T(8,128)(2,1)S(1)}, ...), condition=%wide.while_cond, body=%wide.while_body.sunk | while | flops 163869 | bytes 1638603 | solution.py:136
  316.3 3.2 and_reduce_fusion.2
  322.5 5.6 %dynamic-update-slice.3 = bf16[2,5,2304,128]{3,2,1,0:T(8,128)(2,1)} dynamic-update-slice(bf16[2,5,2304,128]{3,2,1,0:T(8,128)(2,1)} %get-tuple-element.113, bf16[1,5,256,128]{3,2,1,0:T(8,128)(2,1)S(1)} %dynamic-slice_select_fusion.2, s32[]{:T(128)} %bitcast.89, s32[]{:T(128)} %constant.38.clone.1..sunk, s32[]{:T(128)} %bitcast.90, s32[]{:T(128)} %constant.38.clone.1..sunk) | dynamic-update-slice | bytes 655364 | tf_op jit(solution)/shard_map/vmap(vmap())/scatter
  328.7 3.2 and_reduce_fusion.2
  332.0 3.0 dynamic-slice_select_fusion.2
  335.0 5.6 %dynamic-update-slice.3 = bf16[2,5,2304,128]{3,2,1,0:T(8,128)(2,1)} dynamic-update-slice(bf16[2,5,2304,128]{3,2,1,0:T(8,128)(2,1)} %get-tuple-element.113, bf16[1,5,256,128]{3,2,1,0:T(8,128)(2,1)S(1)} %dynamic-slice_select_fusion.2, s32[]{:T(128)} %bitcast.89, s32[]{:T(128)} %constant.38.clone.1..sunk, s32[]{:T(128)} %bitcast.90, s32[]{:T(128)} %constant.38.clone.1..sunk) | dynamic-update-slice | bytes 655364 | tf_op jit(solution)/shard_map/vmap(vmap())/scatter
  344.9 15.9 %collective-permute-done = bf16[2,5,288,128]{3,2,1,0:T(8,128)(2,1)} collective-permute-done((bf16[2,5,288,128]{3,2,1,0:T(8,128)(2,1)}, bf16[2,5,288,128]{3,2,1,0:T(8,128)(2,1)}, u32[]{:S(2)}, u32[]{:S(2)}) %collective-permute-start) | collective-permute-done | bytes 737312 | tf_op jit(solution)/shard_map/ppermute | solution.py:11
  360.8 3.2 maximum_select_fusion
  364.0 30.0 %all-reduce.3.cloned.1.call-done = f32[512,2048]{1,0:T(8,128)} async-done(((f32[512,2048]{1,0:T(8,128)}), f32[512,2048]{1,0:T(8,128)}) %all-reduce.3.cloned.1.call-update) | async-done | bytes 4194320 | tf_op jit(solution)/shard_map/psum | solution.py:128
  394.0 4.2 %fusion.12 = bf16[512,2048]{1,0:T(8,128)(2,1)} fusion(f32[512,2048]{1,0:T(8,128)} %all-reduce.3.cloned.1.call-done, bf16[2,256,2048]{2,1,0:T(8,128)(2,1)S(1)} %copy-done.3), kind=kLoop, calls=%fused_computation.29 | loop fusion | flops 3145728 | bytes 8388608 | tf_op jit(solution)/shard_map/convert_element_type | solution.py:129
  (74 shorter events, 23.7 us)
Async XLA Ops:
  7.2 298.8 %copy-start = (bf16[320,2048]{1,0:T(8,128)(2,1)S(1)}, bf16[320,2048]{1,0:T(8,128)(2,1)}, u32[]{:S(2)}) copy-start(bf16[320,2048]{1,0:T(8,128)(2,1)} %param.17) | copy-start | bytes 3932164
  12.4 7.4 %copy-start.9 = (s32[16]{0:T(128)S(1)}, s32[16]{0:T(128)}, u32[]{:S(2)}) copy-start(s32[16]{0:T(128)} %param.21) | copy-start | bytes 196
  12.4 7.4 %copy-start.12 = (s32[16]{0:T(128)S(1)}, s32[16]{0:T(128)}, u32[]{:S(2)}) copy-start(s32[16]{0:T(128)} %param.22) | copy-start | bytes 196
  12.4 100.7 %all-to-all-start = ((bf16[1,5,2048,128]{3,1,0,2:T(8,128)(2,1)}), bf16[1,5,2048,128]{3,1,0,2:T(8,128)(2,1)}, u32[]{:S(2)}, u32[]{:S(2)}) async-start(bf16[1,5,2048,128]{3,1,0,2:T(8,128)(2,1)} %copy.40), calls=%async_computation | async-start | bytes 8388608 | tf_op jit(solution)/shard_map/all_to_all | solution.py:75
  128.3 119.6 %all-to-all-start.1 = ((bf16[16,5,256,128]{3,2,1,0:T(8,128)(2,1)}), bf16[16,5,256,128]{3,2,1,0:T(8,128)(2,1)}, u32[]{:S(2)}, u32[]{:S(2)}) async-start(bf16[16,5,256,128]{3,2,1,0:T(8,128)(2,1)} %select_select_fusion), calls=%async_computation.1 | async-start | bytes 10485760 | tf_op jit(solution)/shard_map/all_to_all | solution.py:79
  133.0 4.8 %copy-start.2 = (bf16[2,256,2048]{2,1,0:T(8,128)(2,1)S(1)}, bf16[2,256,2048]{2,1,0:T(8,128)(2,1)}, u32[]{:S(2)}) copy-start(bf16[2,256,2048]{2,1,0:T(8,128)(2,1)} %param.13) | copy-start | bytes 6291460
  133.0 261.0 %all-reduce.3.cloned.1.call-start = ((), (), s32[]{:S(2)}) async-start(), calls=%async_computation.2 | async-start | bytes 8388608 | tf_op jit(solution)/shard_map/psum | solution.py:128
  133.2 5.1 %copy-start.15 = (f32[2048]{0:T(1024)S(1)}, f32[2048]{0:T(1024)}, u32[]{:S(2)}) copy-start(f32[2048]{0:T(1024)} %param.14) | copy-start | bytes 24580
  138.3 5.2 %copy-start.13 = (s32[16]{0:T(128)S(1)}, s32[16]{0:T(128)}, u32[]{:S(2)}) copy-start(s32[16]{0:T(128)} %param.23) | copy-start | bytes 196
  141.7 1.1 copy-start.4
  144.9 2.8 copy-start.5
  144.9 2.8 copy-start.10
  144.9 2.8 copy-start.11
  147.3 1.0 copy-start.6
  252.0 4.1 %copy-start.1 = (bf16[2,5,2048,128]{3,2,1,0:T(8,128)(2,1)}, bf16[2,5,2048,128]{3,2,1,0:T(8,128)(2,1)S(1)}, u32[]{:S(2)}) copy-start(bf16[2,5,2048,128]{3,2,1,0:T(8,128)(2,1)S(1)} %bitcast_select_fusion) | copy-start | bytes 15728644
  299.6 6.4 %copy-start.7 = (bf16[5,64,256]{2,1,0:T(8,128)(2,1)S(1)}, bf16[5,64,256]{2,1,0:T(8,128)(2,1)}, u32[]{:S(2)}) copy-start(bf16[5,64,256]{2,1,0:T(8,128)(2,1)} %fusion.37) | copy-start | bytes 491524
  309.3 0.7 copy-start.14
  310.1 5.6 %copy-start.8 = (s32[4]{0:T(128)S(1)}, s32[4]{0:T(128)}, u32[]{:S(2)}) copy-start(s32[4]{0:T(128)} %constant.238) | copy-start | bytes 52
  340.5 53.4 %copy-start.3 = (bf16[2,256,2048]{2,1,0:T(8,128)(2,1)S(1)}, bf16[2,256,2048]{2,1,0:T(8,128)(2,1)}, u32[]{:S(2)}) copy-start(bf16[2,256,2048]{2,1,0:T(8,128)(2,1)} %param.13) | copy-start | bytes 6291460
  343.3 17.6 %collective-permute-start = (bf16[2,5,288,128]{3,2,1,0:T(8,128)(2,1)}, bf16[2,5,288,128]{3,2,1,0:T(8,128)(2,1)}, u32[]{:S(2)}, u32[]{:S(2)}) collective-permute-start(bf16[2,5,288,128]{3,2,1,0:T(8,128)(2,1)} %get-tuple-element.48), channel_id=1, source_target_pairs={{0,4},{4,0},{8,12},{12,8},{16,20},{20,16},{24,28},{28,24},{1,5},{5... | collective-permute-start | bytes 2211848 | tf_op jit(solution)/shard_map/ppermute | solution.py:11
Sparse Core Ops, SparseCore 0:
  309.4 84.5 all-reduce.2
where the time goes:
time: 407 us; the launch traced here: 405 us
  waiting for transfers between devices  236 us (58%)
  local copies, waits for them, and re-layouts  66.8 us (16%)
  other arithmetic  41.1 us (10%)
  matrix products  33 us (8%)
  between operations  14.3 us (4%)
  starting transfers between devices  13.9 us (3%)
    all_to_all x1, waiting for transfers between devices, on_device(): lax.all_to_all(jnp.where(live_all[:, None, None, None], select_chosen, jn...  96.6 us
    all_to_all x1, waiting for transfers between devices, on_device(): lax.all_to_all(stored, 'req', split_axis=2, concat_axis=0, tiled=True)  93.2 us
    psum x1, waiting for transfers between devices, on_device(): lax.psum(jnp.dot(mixed_all, w_out, preferred_element_type=jnp.float32), '...  30 us
    gather x4, local copies, waits for them, and re-layouts, on_device(): chosen = jnp.take(keys_all[number], head_select, axis=0)  20.1 us
    ppermute x1, waiting for transfers between devices, swapped(): return lax.ppermute(value, axis, pairs)  15.9 us
    dot_general x2, matrix products, attend(): jnp.einsum('hqk,hkd->qhd', probs, keys_one[..., head_dim:], preferred_ele...  13.3 us
    scatter x6, local copies, waits for them, and re-layouts  12.4 us
    scatter x4, other arithmetic  12.4 us
  transfers between devices with their start and end apart: 4, of which 4 were waited for; matrix products, arithmetic and copies ran while one was open for 13% of the time, Pallas kernels for 0%

commit v1 on v0

--- a/solution.py
+++ b/solution.py
@@ -125,7 +125,9 @@
         mixed = attend(query_one, chosen, allowed, head_dim, new_count, scale)
         outputs.append(mixed)
     mixed_all = jnp.concatenate(outputs, axis=0)
-    summed = lax.psum(jnp.dot(mixed_all, w_out, preferred_element_type=jnp.float32), "tp")
+    block = jnp.dot(mixed_all, w_out, preferred_element_type=jnp.float32)
+    terms = lax.all_gather(block, "tp")
+    summed = jnp.sum(terms, axis=0)
     layer = (token_rows.astype(jnp.float32) + summed).astype(jnp.bfloat16)
     layer = layer.reshape(req_dev, new_count, width)
     padded_tokens = jnp.concatenate(

time: 407 us -> 438 us (1.076)
  waiting for transfers between devices: 236 us -> 259 us
  other arithmetic: 41.1 us -> 49.8 us
    all_gather x0 -> x1, waiting for transfers between devices: none -> 53.6 us  [on_device(): terms = lax.all_gather(block, 'tp')]
    psum x1 -> x0, waiting for transfers between devices: 30 us -> none  [on_device(): lax.psum(jnp.dot(mixed_all, w_out, preferred_element_type=jnp.float32), '...]
    reduce_sum x0 -> x1, other arithmetic: none -> 10.2 us  [on_device(): summed = jnp.sum(terms, axis=0)]
  transfers between devices with their start and end apart: 4 -> 4, of which waited for: 4 -> 4; matrix products, arithmetic and copies ran while one was open for 13% -> 12% of each run, Pallas kernels for 0% -> 0%
where the time goes in v1:
time: 438 us; the launch traced here: 436 us
  waiting for transfers between devices  259 us (59%)
  local copies, waits for them, and re-layouts  65.9 us (15%)
  other arithmetic  49.8 us (11%)
  matrix products  33.1 us (8%)
  between operations  14.4 us (3%)
  starting transfers between devices  13.6 us (3%)
    all_to_all x1, waiting for transfers between devices, on_device(): lax.all_to_all(jnp.where(live_all[:, None, None, None], select_chosen, jn...  96.6 us
    all_to_all x1, waiting for transfers between devices, on_device(): lax.all_to_all(stored, 'req', split_axis=2, concat_axis=0, tiled=True)  93.2 us
    all_gather x1, waiting for transfers between devices, on_device(): terms = lax.all_gather(block, 'tp')  53.6 us
    gather x4, local copies, waits for them, and re-layouts, on_device(): chosen = jnp.take(keys_all[number], head_select, axis=0)  20 us
    ppermute x1, waiting for transfers between devices, swapped(): return lax.ppermute(value, axis, pairs)  15.6 us
    dot_general x2, matrix products, attend(): jnp.einsum('hqk,hkd->qhd', probs, keys_one[..., head_dim:], preferred_ele...  13.3 us
    scatter x6, local copies, waits for them, and re-layouts  12.5 us
    scatter x4, other arithmetic  12.5 us
  transfers between devices with their start and end apart: 4, of which 4 were waited for; matrix products, arithmetic and copies ran while one was open for 12% of the time, Pallas kernels for 0%

profile of v1, /device:TPU:0, one launch (start us, length us, event | category | flops | bytes accessed | tf_op | source)
XLA Modules:
  0.0 435.9 jit_solution(16942815588735358366)
XLA Ops:
  7.2 5.2 %copy.40 = bf16[1,5,2048,128]{3,1,0,2:T(8,128)(2,1)} copy(bf16[1,5,2048,128]{3,2,1,0:T(8,128)(2,1)} %param.20) | data formatting | bytes 5242880 | tf_op args[7]
  12.4 7.4 %all-to-all-start = ((bf16[1,5,2048,128]{3,1,0,2:T(8,128)(2,1)}), bf16[1,5,2048,128]{3,1,0,2:T(8,128)(2,1)}, u32[]{:S(2)}, u32[]{:S(2)}) async-start(bf16[1,5,2048,128]{3,1,0,2:T(8,128)(2,1)} %copy.40), calls=%async_computation | async-start | bytes 8388608 | tf_op jit(solution)/shard_map/all_to_all | solution.py:75
  19.9 93.2 %all-to-all-done = bf16[1,5,2048,128]{3,1,0,2:T(8,128)(2,1)} async-done(((bf16[1,5,2048,128]{3,1,0,2:T(8,128)(2,1)}), bf16[1,5,2048,128]{3,1,0,2:T(8,128)(2,1)}, u32[]{:S(2)}, u32[]{:S(2)}) %all-to-all-start) | async-done | bytes 2621472 | tf_op jit(solution)/shard_map/all_to_all | solution.py:75
  113.1 4.4 %copy.54 = bf16[1,5,8,256,128]{4,3,1,2,0:T(8,128)(2,1)} copy(bf16[1,5,8,256,128]{4,1,3,2,0:T(8,128)(2,1)} %bitcast) | data formatting | bytes 5242880 | tf_op jit(solution)/shard_map/all_to_all | solution.py:75
  117.6 5.3 %gather_fusion = bf16[16,5,256,128]{3,2,1,0:T(8,128)(2,1)} fusion(bf16[8,5,256,128]{3,2,1,0:T(8,128)(2,1)} %bitcast.92, s32[1024]{0:T(1024)S(1)} %pad_clamp_fusion.1), kind=kCustom, calls=%fused_computation.2 | custom fusion | bytes 10485824 | tf_op jit(solution)/shard_map/jit(_take)/gather | solution.py:78
  122.9 5.5 %select_select_fusion = bf16[16,5,256,128]{3,2,1,0:T(8,128)(2,1)} fusion(bf16[16,5,256,128]{3,2,1,0:T(8,128)(2,1)} %gather_fusion, pred[16]{0:T(512)(128)(4,1)S(1)} %get-tuple-element.41, pred[16]{0:T(512)(128)(4,1)S(1)} %get-tuple-element.65), kind=kLoop, calls=%fused_computation.30 | loop fusion | flops 5242880 | bytes 10485792 | tf_op jit(solution)/shard_map/jit(_where)/select_n | solution.py:80
  128.3 4.6 %all-to-all-start.1 = ((bf16[16,5,256,128]{3,2,1,0:T(8,128)(2,1)}), bf16[16,5,256,128]{3,2,1,0:T(8,128)(2,1)}, u32[]{:S(2)}, u32[]{:S(2)}) async-start(bf16[16,5,256,128]{3,2,1,0:T(8,128)(2,1)} %select_select_fusion), calls=%async_computation.1 | async-start | bytes 10485760 | tf_op jit(solution)/shard_map/all_to_all | solution.py:79
  133.2 4.6 %copy.44 = bf16[2048,640]{0,1:T(8,128)(2,1)} copy(bf16[2048,640]{1,0:T(8,128)(2,1)} %param.16) | data formatting | bytes 5242880 | tf_op args[3]
  138.3 3.4 fusion.48
  151.3 96.6 %all-to-all-done.1 = bf16[16,5,256,128]{3,2,1,0:T(8,128)(2,1)} async-done(((bf16[16,5,256,128]{3,2,1,0:T(8,128)(2,1)}), bf16[16,5,256,128]{3,2,1,0:T(8,128)(2,1)}, u32[]{:S(2)}, u32[]{:S(2)}) %all-to-all-start.1) | async-done | bytes 5242912 | tf_op jit(solution)/shard_map/all_to_all | solution.py:79
  252.0 4.3 fusion.17
  256.2 4.5 %gather_fusion.1 = bf16[5,2304,128]{2,1,0:T(8,128)(2,1)} fusion(bf16[5,2304,128]{2,1,0:T(8,128)(2,1)} %get-tuple-element.49, s32[1024]{0:T(1024)S(1)} %pad_clamp_fusion), kind=kCustom, calls=%fused_computation.clone | custom fusion | bytes 5898260 | tf_op jit(solution)/shard_map/jit(_take)/gather | solution.py:119
  260.8 4.6 %gather_fusion.2 = bf16[5,2304,128]{2,1,0:T(8,128)(2,1)} fusion(bf16[5,2304,128]{2,1,0:T(8,128)(2,1)} %get-tuple-element.50, s32[1024]{0:T(1024)S(1)} %pad_clamp_fusion), kind=kCustom, calls=%fused_computation.1.clone | custom fusion | bytes 5898260 | tf_op jit(solution)/shard_map/jit(_take)/gather | solution.py:119
  265.4 5.4 %copy.47 = bf16[5,2304,128]{1,2,0:T(8,128)(2,1)} copy(bf16[5,2304,128]{2,1,0:T(8,128)(2,1)} %gather_fusion.2) | data formatting | bytes 5898240 | tf_op jit(solution)/shard_map/jit(_take)/gather | solution.py:119
  270.8 5.5 %copy.46 = bf16[5,2304,128]{1,2,0:T(8,128)(2,1)} copy(bf16[5,2304,128]{2,1,0:T(8,128)(2,1)} %gather_fusion.1) | data formatting | bytes 5898240 | tf_op jit(solution)/shard_map/jit(_take)/gather | solution.py:119
  276.2 5.9 %broadcast_select_fusion.1 = (bf16[5,2304,128]{1,2,0:T(8,128)(2,1)}, bf16[5,2304,128]{1,2,0:T(8,128)(2,1)}) fusion(bf16[5,2304,128]{1,2,0:T(8,128)(2,1)} %copy.46, pred[5]{0:T(512)(128)(4,1)S(1)} %compare_and_fusion, bf16[5,2304,128]{1,2,0:T(8,128)(2,1)} %copy.47), kind=kLoop, calls=%fused_computation.40 | loop fusion | flops 2949120 | bytes 11796485 | tf_op jit(solution)/shard_map/jit(_take)/select_n | solution.py:119
  282.1 5.2 %fusion.98 = f32[5,256]{1,0:T(8,128)S(1)} fusion(pred[256,2304]{1,0:T(8,128)(4,1)S(1)} %get-tuple-element.57, bf16[5,2304,128]{1,2,0:T(8,128)(2,1)} %get-tuple-element.61, bf16[2,256,5,32]{1,3,2,0:T(8,128)(2,1)S(1)} %get-tuple-element.51, bf16[2,256,5,32]{1,3,2,0:T(8,128)(2,1)S(1)} %get-tuple-element.52), kind=kOutput, calls=%fused_computation.123 | convolution fusion | flops 389613824 | bytes 2397184 | tf_op jit(solution)/shard_map/sub | solution.py:43
  287.3 7.0 %fusion.43 = bf16[5,64,256]{2,1,0:T(8,128)(2,1)} fusion(f32[5,256]{1,0:T(8,128)S(1)} %fusion.98, bf16[5,2304,128]{1,2,0:T(8,128)(2,1)} %get-tuple-element.61, pred[256,2304]{1,0:T(8,128)(4,1)S(1)} %get-tuple-element.57, bf16[2,256,5,32]{1,3,2,0:T(8,128)(2,1)S(1)} %get-tuple-element.51, bf16[2,256,5,32]{1,3,2,0:T(8,128)(2,1)S(1)} %get-tuple-element.52), kind=kOutput, calls=%fused_computation.58 | convolution fusion | flops 770133504 | bytes 4035584 | tf_op jit(solution)/shard_map/hqk,hkd->qhd/dot_general | solution.py:45
  294.3 5.5 %fusion.93 = f32[5,256]{1,0:T(8,128)S(1)} fusion(pred[256,2304]{1,0:T(8,128)(4,1)S(1)} %get-tuple-element.58, bf16[5,2304,128]{1,2,0:T(8,128)(2,1)} %get-tuple-element.62, bf16[2,256,5,32]{1,3,2,0:T(8,128)(2,1)S(1)} %get-tuple-element.52, bf16[2,256,5,32]{1,3,2,0:T(8,128)(2,1)S(1)} %get-tuple-element.51), kind=kOutput, calls=%fused_computation.122 | convolution fusion | flops 389613824 | bytes 2397184 | tf_op jit(solution)/shard_map/sub | solution.py:43
  299.8 6.3 %fusion.40 = bf16[5,64,256]{2,1,0:T(8,128)(2,1)S(1)} fusion(f32[5,256]{1,0:T(8,128)S(1)} %fusion.93, bf16[5,2304,128]{1,2,0:T(8,128)(2,1)} %get-tuple-element.62, pred[256,2304]{1,0:T(8,128)(4,1)S(1)} %get-tuple-element.58, bf16[2,256,5,32]{1,3,2,0:T(8,128)(2,1)S(1)} %get-tuple-element.52, bf16[2,256,5,32]{1,3,2,0:T(8,128)(2,1)S(1)} %get-tuple-element.51), kind=kOutput, calls=%fused_computation.57 | convolution fusion | flops 770133504 | bytes 4035584 | tf_op jit(solution)/shard_map/hqk,hkd->qhd/dot_general | solution.py:45
  306.1 3.3 fusion.50
  310.3 5.9 %concatenate.30 = bf16[2,5,2304,128]{3,2,1,0:T(8,128)(2,1)} pad(bf16[2,5,2048,128]{3,2,1,0:T(8,128)(2,1)} %copy-done.1, bf16[]{:T(256)} %constant.52.clone.1), padding=0_0x0_0x0_256x0_0 | pad | bytes 11141122 | tf_op jit(solution)/shard_map/concatenate | solution.py:133
  316.3 25.0 %while.1 = (s32[]{:T(128)}, bf16[2,5,2304,128]{3,2,1,0:T(8,128)(2,1)}, s32[2,4]{1,0:T(2,128)S(1)}, bf16[2,5,256,128]{3,2,1,0:T(8,128)(2,1)S(1)}, s32[]{:T(128)}, /*index=5*/s32[4]{0:T(128)S(1)}, s32[]{:T(128)}) while((s32[]{:T(128)}, bf16[2,5,2304,128]{3,2,1,0:T(8,128)(2,1)}, s32[2,4]{1,0:T(2,128)S(1)}, bf16[2,5,256,128]{3,2,1,0:T(8,128)(2,1)S(1)}, ...), condition=%wide.while_cond, body=%wide.while_body.sunk | while | flops 163869 | bytes 1638603 | solution.py:138
  316.9 3.3 and_reduce_fusion.2
  323.1 5.7 %dynamic-update-slice.3 = bf16[2,5,2304,128]{3,2,1,0:T(8,128)(2,1)} dynamic-update-slice(bf16[2,5,2304,128]{3,2,1,0:T(8,128)(2,1)} %get-tuple-element.113, bf16[1,5,256,128]{3,2,1,0:T(8,128)(2,1)S(1)} %dynamic-slice_select_fusion.2, s32[]{:T(128)} %bitcast.86, s32[]{:T(128)} %constant.38.clone.1..sunk, s32[]{:T(128)} %bitcast.87, s32[]{:T(128)} %constant.38.clone.1..sunk) | dynamic-update-slice | bytes 655364 | tf_op jit(solution)/shard_map/vmap(vmap())/scatter
  329.4 3.2 and_reduce_fusion.2
  332.7 3.0 dynamic-slice_select_fusion.2
  335.7 5.6 %dynamic-update-slice.3 = bf16[2,5,2304,128]{3,2,1,0:T(8,128)(2,1)} dynamic-update-slice(bf16[2,5,2304,128]{3,2,1,0:T(8,128)(2,1)} %get-tuple-element.113, bf16[1,5,256,128]{3,2,1,0:T(8,128)(2,1)S(1)} %dynamic-slice_select_fusion.2, s32[]{:T(128)} %bitcast.86, s32[]{:T(128)} %constant.38.clone.1..sunk, s32[]{:T(128)} %bitcast.87, s32[]{:T(128)} %constant.38.clone.1..sunk) | dynamic-update-slice | bytes 655364 | tf_op jit(solution)/shard_map/vmap(vmap())/scatter
  344.1 15.6 %collective-permute-done = bf16[2,5,288,128]{3,2,1,0:T(8,128)(2,1)S(1)} collective-permute-done((bf16[2,5,288,128]{3,2,1,0:T(8,128)(2,1)S(1)}, bf16[2,5,288,128]{3,2,1,0:T(8,128)(2,1)S(1)}, u32[]{:S(2)}, u32[]{:S(2)}) %collective-permute-start) | collective-permute-done | bytes 737312 | tf_op jit(solution)/shard_map/ppermute | solution.py:11
  361.0 53.6 %all-gather.3.cloned.1.call-done = f32[2048,2048]{1,0:T(8,128)} async-done(((f32[512,2048]{1,0:T(8,128)}), f32[2048,2048]{1,0:T(8,128)}) %all-gather.3.cloned.1.call-update) | async-done | bytes 16777232 | tf_op jit(solution)/shard_map/all_gather | solution.py:129
  414.6 10.2 %reduce_sum.61 = f32[512,2048]{1,0:T(8,128)} reduce(f32[4,512,2048]{2,1,0:T(8,128)} %bitcast.93, f32[]{:T(128)} %constant.53.clone.1), dimensions={0}, to_apply=%region_7.9 | reduce | flops 3145728 | bytes 20971524 | tf_op jit(solution)/shard_map/reduce_sum | solution.py:130
  424.9 4.2 fusion.15
  (75 shorter events, 23.4 us)
Async XLA Ops:
  7.2 299.0 %copy-start = (bf16[320,2048]{1,0:T(8,128)(2,1)S(1)}, bf16[320,2048]{1,0:T(8,128)(2,1)}, u32[]{:S(2)}) copy-start(bf16[320,2048]{1,0:T(8,128)(2,1)} %param.17) | copy-start | bytes 3932164
  12.4 7.4 %copy-start.9 = (s32[16]{0:T(128)S(1)}, s32[16]{0:T(128)}, u32[]{:S(2)}) copy-start(s32[16]{0:T(128)} %param.21) | copy-start | bytes 196
  12.4 7.4 %copy-start.12 = (s32[16]{0:T(128)S(1)}, s32[16]{0:T(128)}, u32[]{:S(2)}) copy-start(s32[16]{0:T(128)} %param.22) | copy-start | bytes 196
  12.4 100.7 %all-to-all-start = ((bf16[1,5,2048,128]{3,1,0,2:T(8,128)(2,1)}), bf16[1,5,2048,128]{3,1,0,2:T(8,128)(2,1)}, u32[]{:S(2)}, u32[]{:S(2)}) async-start(bf16[1,5,2048,128]{3,1,0,2:T(8,128)(2,1)} %copy.40), calls=%async_computation | async-start | bytes 8388608 | tf_op jit(solution)/shard_map/all_to_all | solution.py:75
  128.3 119.6 %all-to-all-start.1 = ((bf16[16,5,256,128]{3,2,1,0:T(8,128)(2,1)}), bf16[16,5,256,128]{3,2,1,0:T(8,128)(2,1)}, u32[]{:S(2)}, u32[]{:S(2)}) async-start(bf16[16,5,256,128]{3,2,1,0:T(8,128)(2,1)} %select_select_fusion), calls=%async_computation.1 | async-start | bytes 10485760 | tf_op jit(solution)/shard_map/all_to_all | solution.py:79
  133.0 4.8 %copy-start.2 = (bf16[2,256,2048]{2,1,0:T(8,128)(2,1)S(1)}, bf16[2,256,2048]{2,1,0:T(8,128)(2,1)}, u32[]{:S(2)}) copy-start(bf16[2,256,2048]{2,1,0:T(8,128)(2,1)} %param.13) | copy-start | bytes 6291460
  133.0 281.6 %all-gather.3.cloned.1.call-start = ((), (), s32[]{:S(2)}) async-start(), calls=%async_computation.2 | async-start | bytes 20971520 | tf_op jit(solution)/shard_map/all_gather | solution.py:129
  133.2 5.1 %copy-start.15 = (f32[2048]{0:T(1024)S(1)}, f32[2048]{0:T(1024)}, u32[]{:S(2)}) copy-start(f32[2048]{0:T(1024)} %param.14) | copy-start | bytes 24580
  138.3 5.2 %copy-start.13 = (s32[16]{0:T(128)S(1)}, s32[16]{0:T(128)}, u32[]{:S(2)}) copy-start(s32[16]{0:T(128)} %param.23) | copy-start | bytes 196
  141.7 1.1 copy-start.4
  144.9 2.8 copy-start.5
  144.9 2.8 copy-start.10
  144.9 2.8 copy-start.11
  147.3 1.0 copy-start.6
  252.0 4.3 copy-start.1
  299.8 6.4 %copy-start.7 = (bf16[5,64,256]{2,1,0:T(8,128)(2,1)S(1)}, bf16[5,64,256]{2,1,0:T(8,128)(2,1)}, u32[]{:S(2)}) copy-start(bf16[5,64,256]{2,1,0:T(8,128)(2,1)} %fusion.43) | copy-start | bytes 491524
  309.5 0.7 copy-start.14
  310.3 5.9 %copy-start.8 = (s32[4]{0:T(128)S(1)}, s32[4]{0:T(128)}, u32[]{:S(2)}) copy-start(s32[4]{0:T(128)} %constant.241) | copy-start | bytes 52
  342.7 16.9 %collective-permute-start = (bf16[2,5,288,128]{3,2,1,0:T(8,128)(2,1)S(1)}, bf16[2,5,288,128]{3,2,1,0:T(8,128)(2,1)S(1)}, u32[]{:S(2)}, u32[]{:S(2)}) collective-permute-start(bf16[2,5,288,128]{3,2,1,0:T(8,128)(2,1)S(1)} %get-tuple-element.48), channel_id=1, source_target_pairs={{0,4},{4,0},{8,12},{12,8},{16,20},{20,16},{24,28},{28,24},{1,5},{5... | collective-permute-start | bytes 2211848 | tf_op jit(solution)/shard_map/ppermute | solution.py:11
  414.6 10.2 %copy-start.3 = (bf16[2,256,2048]{2,1,0:T(8,128)(2,1)S(1)}, bf16[2,256,2048]{2,1,0:T(8,128)(2,1)}, u32[]{:S(2)}) copy-start(bf16[2,256,2048]{2,1,0:T(8,128)(2,1)} %param.13) | copy-start | bytes 6291460
Sparse Core Ops, SparseCore 0:
  309.6 104.9 all-gather.2
